TPU v7x, 32 devices: a whole 2x2x4 slice. The times are simulated.
32 devices in a mesh: tower: 4 (over y, x), member: 8 (over z, core).
Axes of the slice: x: 2, y: 2, z: 4, core: 2. Of those that a mesh axis runs over, the one named last changes fastest.
Arguments:
- bag_ids: int32 [8, 8, 4, 512], P('tower', 'member'), may hold values from 0 to 511
- touch_ids: int32 [8, 8, 128], P('tower', 'member'), may hold values from 0 to 511, as said below
- elapsed: int32 [8, 8, 128], P('tower', 'member'), may hold values from 0 to 39
- tables: float32 [8, 8, 512, 64], P('tower', 'member'), may hold values from -3 to 3
- accumulator: float32 [8, 8, 512], P('tower', 'member'), may hold values from 0.001 to 0.1
- first_weight: float32 [512, 8, 1024], P(None, 'tower'), may hold values from -0.25 to 0.25
- second_weight: float32 [1024, 8, 256], P(None, 'tower'), may hold values from -0.1875 to 0.1875
- lift_weight: float32 [2048, 128], replicated, may hold values from -0.5 to 0.5
- press_weight: float32 [2048, 128], replicated, may hold values from -0.125 to 0.125
- head_weight: float32 [2048], replicated, may hold values from -0.125 to 0.125
- labels: int32 [8, 64], P('member'), may hold values 0 or 1
Outputs:
- new_tables: float32 [8, 8, 512, 64], P('tower', 'member')
- new_accumulator: float32 [8, 8, 512], P('tower', 'member')
- grad_first: float32 [512, 8, 1024], P('member', 'tower')
- grad_second: float32 [1024, 8, 256], P('member', 'tower')
- grad_lift: float32 [2048, 128], P(('tower', 'member'))
- grad_press: float32 [2048, 128], P(('tower', 'member'))
- logits: float32 [8, 64], P('member', 'tower')
Inputs may be any that keep to these rules, and one draw needn't show every extreme that they name: `touch_ids`: distinct within each table.
All inputs are finite; a program needn't handle non-finite values. No bound on the sum of `labels` on one device may be relied on, other than what follows from the above.
Results may differ from a plain program's by a relative error of at most 0.0003.
Values sent between devices are 32-bit elements; how exact they have to be, the bound alone decides.
A program may use at most 128 MiB of HBM per device.

v0:
```python
import math

import jax
import jax.numpy as jnp
from jax import lax
from jax.sharding import PartitionSpec as P

PRECISE = lax.Precision.HIGHEST
DECAY_RATE = 0.98
LEARN_RATE = 1.0
EPSILON = 1e-08


def decay_factors(touch_ids, elapsed, table_rows):
    rates = jnp.exp(elapsed.astype(jnp.float32) * math.log(DECAY_RATE))
    matches = touch_ids[..., None] == jnp.arange(table_rows, dtype=jnp.int32)
    hits = jnp.sum(matches.astype(jnp.float32), axis=-2)
    chosen = jnp.sum(jnp.where(matches, rates[..., None], jnp.float32(0.0)), axis=-2)
    return jnp.where(hits > 0.0, chosen, jnp.float32(1.0))


def bag_counts(bag_block, table_rows):
    matches = bag_block[..., None] == jnp.arange(table_rows, dtype=jnp.int32)
    return jnp.sum(matches.astype(jnp.float32), axis=1)


def per_device(
    bag_ids,
    touch_ids,
    elapsed,
    tables,
    accumulator,
    first_weight,
    second_weight,
    lift_weight,
    press_weight,
    head_weight,
    labels,
):
    table_rows = tables.shape[2]
    factors = decay_factors(touch_ids[:, 0], elapsed[:, 0], table_rows)
    decayed = tables[:, 0] * factors[..., None]
    local_bags = bag_ids[:, 0]
    towers_here = local_bags.shape[0]
    bag_size = local_bags.shape[1]
    all_samples = local_bags.shape[2]
    block_size = min(1024, all_samples)
    block_count = all_samples // block_size
    bag_blocks = jnp.transpose(
        local_bags.reshape(towers_here, bag_size, block_count, block_size), (2, 0, 1, 3)
    )

    def pool_block(bag_block):
        return jnp.einsum(
            "tbr,trw->btw", bag_counts(bag_block, table_rows), decayed, precision=PRECISE
        )

    pooled = lax.map(pool_block, bag_blocks).reshape(all_samples, towers_here, -1)
    features = lax.all_to_all(pooled, "member", split_axis=0, concat_axis=2, tiled=True)
    hidden = jnp.einsum("sti,ith->sth", features, first_weight, precision=PRECISE)
    activated = jax.nn.silu(hidden)
    tower_out = jnp.einsum("sth,hto->sto", activated, second_weight, precision=PRECISE)
    samples = tower_out.shape[0]
    flat_out = tower_out.reshape(samples, -1)
    tower_pos = lax.axis_index("tower")
    rank = lift_weight.shape[1]
    width = flat_out.shape[1]
    lift_local = lax.dynamic_slice_in_dim(lift_weight, tower_pos * width, width, 0)
    press_local = lax.dynamic_slice_in_dim(press_weight, tower_pos * width, width, 0)
    head_local = lax.dynamic_slice_in_dim(head_weight, tower_pos * width, width, 0)
    projected = lax.psum(jnp.dot(flat_out, press_local, precision=PRECISE), "tower")
    scaling = jnp.dot(projected, lift_local.T, precision=PRECISE)
    crossed = flat_out * scaling + flat_out
    logit_values = lax.psum(jnp.dot(crossed, head_local, precision=PRECISE), "tower")
    errors = jax.nn.sigmoid(logit_values) - labels[0].astype(jnp.float32)
    grad_crossed = errors[:, None] * head_local[None, :]
    grad_scaling = grad_crossed * flat_out
    grad_projected = lax.psum(jnp.dot(grad_scaling, lift_local, precision=PRECISE), "tower")
    grad_flat = grad_crossed * (scaling + 1.0) + jnp.dot(
        grad_projected, press_local.T, precision=PRECISE
    )
    grad_pair = lax.psum_scatter(
        jnp.concatenate(
            [
                jnp.dot(grad_scaling.T, projected, precision=PRECISE),
                jnp.dot(flat_out.T, grad_projected, precision=PRECISE),
            ],
            axis=1,
        ),
        "member",
        scatter_dimension=0,
        tiled=True,
    )
    owned = samples // lax.axis_size("tower")
    logits_out = lax.dynamic_slice_in_dim(logit_values, tower_pos * owned, owned, 0)[None, :]
    grad_lift = grad_pair[:, :rank]
    grad_press = grad_pair[:, rank:]
    grad_out = grad_flat.reshape(samples, towers_here, -1)
    grad_act = jnp.einsum("sto,hto->sth", grad_out, second_weight, precision=PRECISE)
    sigmoid_hidden = jax.nn.sigmoid(hidden)
    grad_hidden = grad_act * (sigmoid_hidden * (1.0 + hidden * (1.0 - sigmoid_hidden)))
    piece = features
    grad_first = lax.psum_scatter(
        jnp.einsum("sti,sth->ith", piece, grad_hidden, precision=PRECISE),
        "member",
        scatter_dimension=0,
        tiled=True,
    )
    piece = activated
    grad_second = lax.psum_scatter(
        jnp.einsum("sth,sto->hto", piece, grad_out, precision=PRECISE),
        "member",
        scatter_dimension=0,
        tiled=True,
    )
    grad_features = jnp.einsum("sth,ith->sti", grad_hidden, first_weight, precision=PRECISE)
    grad_pooled = lax.all_to_all(grad_features, "member", split_axis=2, concat_axis=0, tiled=True)
    grad_blocks = grad_pooled.reshape(block_count, block_size, towers_here, -1)

    def add_block(total, inputs):
        bag_block, grad_block = inputs
        counts = bag_counts(bag_block, table_rows)
        return (total + jnp.einsum("tbr,btw->trw", counts, grad_block, precision=PRECISE), None)

    grad_tables, unused = lax.scan(add_block, jnp.zeros_like(decayed), (bag_blocks, grad_blocks))
    mean_square = jnp.mean(grad_tables * grad_tables, axis=-1)
    new_accumulator = accumulator[:, 0] + mean_square
    new_tables = decayed - LEARN_RATE * grad_tables / (
        jnp.sqrt(new_accumulator)[..., None] + EPSILON
    )
    return (
        new_tables[:, None],
        new_accumulator[:, None],
        grad_first,
        grad_second,
        grad_lift,
        grad_press,
        logits_out,
    )


def solution(mesh):
    placed = (
        P("tower", "member", None, None),
        P("tower", "member", None),
        P("tower", "member", None),
        P("tower", "member", None, None),
        P("tower", "member", None),
        P(None, "tower", None),
        P(None, "tower", None),
        P(),
        P(),
        P(),
        P("member", None),
    )
    return jax.shard_map(
        per_device,
        mesh=mesh,
        in_specs=placed,
        out_specs=(
            P("tower", "member", None, None),
            P("tower", "member", None),
            P("member", "tower", None),
            P("member", "tower", None),
            P(("tower", "member"), None),
            P(("tower", "member"), None),
            P("member", "tower"),
        ),
        check_vma=False,
    )
```

profile of v0, /device:TPU:0, one launch (start us, length us, event | category | flops | bytes accessed | tf_op | source)
XLA Modules:
  0.0 263.0 jit_solution(13075587831894397850)
XLA Ops:
  8.0 1.9 convert_reduce_fusion
  11.3 2.1 convolution_bitcast_fusion.2
  15.0 6.4 %all-to-all-start = ((f32[8,1,8192]{2,1,0:T(1,128)}), f32[8,1,8192]{2,1,0:T(1,128)S(1)}, u32[]{:S(2)}, u32[]{:S(2)}) async-start(f32[8,1,8192]{2,1,0:T(1,128)} %reshape.76), calls=%async_computation | async-start | bytes 524288 | tf_op jit(solution)/shard_map/all_to_all | solution.py:59
  22.2 8.9 %all-to-all-done = f32[8,1,8192]{2,1,0:T(1,128)S(1)} async-done(((f32[8,1,8192]{2,1,0:T(1,128)}), f32[8,1,8192]{2,1,0:T(1,128)S(1)}, u32[]{:S(2)}, u32[]{:S(2)}) %all-to-all-start) | async-done | bytes 262176 | tf_op jit(solution)/shard_map/all_to_all | solution.py:59
  33.7 5.9 %fusion.14 = f32[64,2,1024]{2,0,1:T(8,128)S(1)} fusion(f32[64,2,512]{2,0,1:T(8,128)S(1)} %all_to_all.27, f32[512,2,1024]{2,1,0:T(2,128)} %param.16), kind=kOutput, calls=%fused_computation.14 | convolution fusion | flops 805306368 | bytes 4980736 | tf_op jit(solution)/shard_map/sti,ith->sth/dot_general | solution.py:60
  39.6 1.5 fusion.20
  42.4 16.3 %psum.21 = f32[64,128]{1,0:T(8,128)S(1)} all-reduce(f32[64,128]{1,0:T(8,128)S(1)} %fusion.29), channel_id=1, replica_groups=mesh['tower'=4,'member'=8] {'tower'}, use_global_device_ids=true, to_apply=%region_3.4 | all-reduce | flops 8192 | bytes 65536 | tf_op jit(solution)/shard_map/psum | solution.py:71
  58.7 1.3 fusion.26
  60.2 8.0 %psum.22 = f32[64]{0:T(128)S(1)} all-reduce(f32[64]{0:T(128)S(1)} %convolution_bitcast_fusion.3), channel_id=1, replica_groups=mesh['tower'=4,'member'=8] {'tower'}, use_global_device_ids=true, to_apply=%region_4.5 | all-reduce | flops 64 | bytes 512 | tf_op jit(solution)/shard_map/psum | solution.py:74
  70.7 15.3 %psum.23 = f32[64,128]{1,0:T(8,128)S(1)} all-reduce(f32[64,128]{1,0:T(8,128)S(1)} %fusion.24), channel_id=1, replica_groups=mesh['tower'=4,'member'=8] {'tower'}, use_global_device_ids=true, to_apply=%region_5.6 | all-reduce | flops 8192 | bytes 65536 | tf_op jit(solution)/shard_map/psum | solution.py:78
  89.1 1.4 convolution_add_fusion
  90.5 2.1 fusion.11
  92.6 5.1 %convolution_bitcast_fusion = f32[512,2,1024]{0,2,1:T(8,128)} fusion(f32[64,2,1024]{2,0,1:T(8,128)S(1)} %fusion.11, f32[64,2,512]{2,0,1:T(8,128)S(1)} %all_to_all.27), kind=kOutput, calls=%fused_computation.6 | convolution fusion | flops 805306368 | bytes 4980736 | tf_op jit(solution)/shard_map/sti,sth->ith/dot_general | solution.py:104
  97.7 7.4 %copy.71 = f32[512,2,1024]{2,1,0:T(2,128)} copy(f32[512,2,1024]{0,2,1:T(8,128)} %convolution_bitcast_fusion) | data formatting | bytes 8388608 | tf_op jit(solution)/shard_map/sti,sth->ith/transpose | solution.py:104
  105.2 3.1 %convolution_bitcast_fusion.1 = f32[1024,2,256]{0,2,1:T(8,128)} fusion(f32[8,2,8,256]{3,2,1,0:T(8,128)S(1)} %bitcast.94, f32[64,2,1024]{2,0,1:T(8,128)S(1)} %fusion.14), kind=kOutput, calls=%fused_computation.11 | convolution fusion | flops 403177472 | bytes 2752512 | tf_op jit(solution)/shard_map/sth,sto->hto/dot_general | solution.py:111
  108.3 7.1 %fusion.17 = f32[64,2,512]{2,0,1:T(8,128)S(1)} fusion(f32[64,2,1024]{2,0,1:T(8,128)S(1)} %fusion.11, f32[512,2,1024]{2,1,0:T(2,128)} %param.16), kind=kOutput, calls=%fused_computation.15 | convolution fusion | flops 805306368 | bytes 4980736 | tf_op jit(solution)/shard_map/sth,ith->sti/dot_general | solution.py:116
  116.9 3.6 %all-to-all-start.1 = ((f32[8,1,8192]{2,1,0:T(1,128)}), f32[8,1,8192]{2,1,0:T(1,128)S(1)}, u32[]{:S(2)}, u32[]{:S(2)}) async-start(f32[8,1,8192]{2,1,0:T(1,128)} %reshape.78), calls=%async_computation.1 | async-start | bytes 524288 | tf_op jit(solution)/shard_map/all_to_all | solution.py:117
  122.4 9.1 %all-to-all-done.1 = f32[8,1,8192]{2,1,0:T(1,128)S(1)} async-done(((f32[8,1,8192]{2,1,0:T(1,128)}), f32[8,1,8192]{2,1,0:T(1,128)S(1)}, u32[]{:S(2)}, u32[]{:S(2)}) %all-to-all-start.1) | async-done | bytes 262176 | tf_op jit(solution)/shard_map/all_to_all | solution.py:117
  133.6 3.1 %multiply_reduce_fusion = (f32[2,512]{1,0:T(2,128)S(1)}, f32[2,512,64]{1,2,0:T(8,128)S(1)}) fusion(f32[2,512,512]{2,1,0:T(8,128)} %copy-done.1, f32[512,2,64]{0,2,1:T(8,128)S(1)} %squeeze.19), kind=kOutput, calls=%fused_computation.30 | convolution fusion | flops 402783232 | bytes 2625536 | tf_op jit(solution)/shard_map/while/body/eval_jaxpr/tbr,btw->trw/dot_general | solution.py:123
  138.1 1.4 fusion.51
  139.5 76.8 %all-reduce.3.cloned.1.call-done = f32[512,2,1024]{2,1,0:T(2,128)} async-done(((f32[512,2,1024]{2,1,0:T(2,128)}), f32[512,2,1024]{2,1,0:T(2,128)}) %all-reduce.3.cloned.1.call-update) | async-done | bytes 4194320
  216.3 1.9 constant_dynamic-slice_fusion
  218.2 36.6 %reduce-scatter.5.cloned.1.call-done = f32[128,2,256]{0,2,1:T(8,128)} async-done(((f32[1024,2,256]{0,2,1:T(8,128)}), f32[128,2,256]{0,2,1:T(8,128)}) %reduce-scatter.5.cloned.1.call-update) | async-done | bytes 262160 | tf_op jit(solution)/shard_map/reduce_scatter | solution.py:110
  254.7 1.8 copy.74
  (60 shorter events, 20.3 us)
Async XLA Ops:
  7.2 32.4 %copy-start = (f32[1024,2,256]{2,1,0:T(2,128)S(1)}, f32[1024,2,256]{2,1,0:T(2,128)}, u32[]{:S(2)}) copy-start(f32[1024,2,256]{2,1,0:T(2,128)} %param.17) | copy-start | bytes 6291460
  7.2 2.8 %copy-start.8 = (s32[2,1,128]{2,1,0:T(1,128)S(1)}, s32[2,1,128]{2,1,0:T(1,128)}, u32[]{:S(2)}) copy-start(s32[2,1,128]{2,1,0:T(1,128)} %param.12) | copy-start | bytes 3076
  7.2 4.2 %copy-start.4 = (f32[2,1,512,64]{2,3,1,0:T(8,128)S(1)}, f32[2,1,512,64]{2,3,1,0:T(8,128)}, u32[]{:S(2)}) copy-start(f32[2,1,512,64]{2,3,1,0:T(8,128)} %param.14) | copy-start | bytes 786436
  9.9 1.4 copy-start.1
  15.0 16.1 %all-to-all-start = ((f32[8,1,8192]{2,1,0:T(1,128)}), f32[8,1,8192]{2,1,0:T(1,128)S(1)}, u32[]{:S(2)}, u32[]{:S(2)}) async-start(f32[8,1,8192]{2,1,0:T(1,128)} %reshape.76), calls=%async_computation | async-start | bytes 524288 | tf_op jit(solution)/shard_map/all_to_all | solution.py:59
  21.3 116.8 %reduce-scatter.7.cloned.1.call-start = ((), (), s32[]{:S(2)}) async-start(), calls=%async_computation.5 | async-start | bytes 589824
  39.6 28.7 %copy-start.9 = (s32[1,64]{1,0:T(1,128)S(1)}, s32[1,64]{1,0:T(1,128)}, u32[]{:S(2)}) copy-start(s32[1,64]{1,0:T(1,128)} %param.21) | copy-start | bytes 772
  60.0 26.0 %copy-start.2 = (f32[64,512]{1,0:T(8,128)}, f32[64,512]{1,0:T(8,128)S(1)}, u32[]{:S(2)}) copy-start(f32[64,512]{1,0:T(8,128)S(1)} %fusion.26) | copy-start | bytes 393220
  86.0 0.6 copy-start.6
  87.0 2.1 copy-start.3
  89.1 127.2 %all-reduce.3.cloned.1.call-start = ((), (), s32[]{:S(2)}) async-start(), calls=%async_computation.6 | async-start | bytes 8388608
  105.1 149.6 %reduce-scatter.5.cloned.1.call-start = ((), (), s32[]{:S(2)}) async-start(), calls=%async_computation.4 | async-start | bytes 2359296 | tf_op jit(solution)/shard_map/reduce_scatter | solution.py:110
  115.4 5.2 %copy-start.10 = (u32[32]{0:T(128)S(1)}, u32[32]{0:T(128)}, u32[]{:S(2)}) copy-start(u32[32]{0:T(128)} %constant.63) | copy-start | bytes 388
  116.9 14.5 %all-to-all-start.1 = ((f32[8,1,8192]{2,1,0:T(1,128)}), f32[8,1,8192]{2,1,0:T(1,128)S(1)}, u32[]{:S(2)}, u32[]{:S(2)}) async-start(f32[8,1,8192]{2,1,0:T(1,128)} %reshape.78), calls=%async_computation.1 | async-start | bytes 524288 | tf_op jit(solution)/shard_map/all_to_all | solution.py:117
  133.1 3.6 %copy-start.7 = (f32[2,1,512]{2,1,0:T(1,128)S(1)}, f32[2,1,512]{2,1,0:T(1,128)}, u32[]{:S(2)}) copy-start(f32[2,1,512]{2,1,0:T(1,128)} %param.15) | copy-start | bytes 12292
  133.1 4.2 %copy-start.5 = (f32[2,1,512,64]{2,3,1,0:T(8,128)S(1)}, f32[2,1,512,64]{2,3,1,0:T(8,128)}, u32[]{:S(2)}) copy-start(f32[2,1,512,64]{2,3,1,0:T(8,128)} %param.14) | copy-start | bytes 786436
Sparse Core Ops, SparseCore 0:
  89.2 29.1 reduce-scatter.6
  120.8 95.4 all-reduce.2
  218.6 36.0 reduce-scatter.4
where the time goes:
time: 264 us; the launch traced here: 263 us
  waiting for transfers between devices  131 us (50%)
  blocking collectives  39.6 us (15%)
  matrix products  37 us (14%)
  local copies, waits for them, and re-layouts  22.4 us (8%)
  between operations  14.7 us (6%)
  starting transfers between devices  10.1 us (4%)
  other arithmetic  7.83 us (3%)
    unnamed x5, waiting for transfers between devices  76.8 us
    reduce_scatter x1, waiting for transfers between devices, per_device(): lax.psum_scatter(jnp.einsum('sth,sto->hto', piece, grad_out, precision=PR...  36.6 us
    psum x1, blocking collectives, per_device(): lax.psum(jnp.dot(flat_out, press_local, precision=PRECISE), 'tower')  16.3 us
    psum x1, blocking collectives, per_device(): lax.psum(jnp.dot(grad_scaling, lift_local, precision=PRECISE), 'tower')  15.3 us
    unnamed x30, local copies, waits for them, and re-layouts  10.4 us
    all_to_all x1, waiting for transfers between devices, per_device(): lax.all_to_all(grad_features, 'member', split_axis=2, concat_axis=0, tile...  9.06 us
    all_to_all x1, waiting for transfers between devices, per_device(): lax.all_to_all(pooled, 'member', split_axis=0, concat_axis=2, tiled=True)  8.9 us
    psum x1, blocking collectives, per_device(): lax.psum(jnp.dot(crossed, head_local, precision=PRECISE), 'tower')  8.04 us
  transfers between devices with their start and end apart: 5, of which 4 were waited for; matrix products, arithmetic and copies ran while one was open for 15% of the time, Pallas kernels for 0%

commit v1 on v0

v1 whole, which is shorter than its diff:
```python
import functools
import math

import jax
import jax.numpy as jnp
from jax import lax
from jax.experimental import pallas as pl
from jax.experimental.pallas import tpu as pltpu
from jax.sharding import PartitionSpec as P

MESH = pl.DeviceIdType.MESH
DECAY_RATE = 0.98
LEARN_RATE = 1.0
EPSILON = 1e-08
F32 = jnp.float32
BF16 = jnp.bfloat16
NN = (((1,), (0,)), ((), ()))
NT = (((1,), (1,)), ((), ()))


def split(x):
    hi = x.astype(BF16)
    return hi, (x - hi.astype(F32)).astype(BF16)


def dot1(a, b, dims=NN):
    return lax.dot_general(a, b, dims, preferred_element_type=F32)


def dot3(a, b, dims=NN):
    (ah, al), (bh, bl) = a, b
    return dot1(ah, bh, dims) + (dot1(ah, bl, dims) + dot1(al, bh, dims))


def sigmoid(x):
    return 1.0 / (1.0 + jnp.exp(-x))


def kernel(
    dims,
    bag_ref,
    touch_ref,
    elapsed_ref,
    tables_ref,
    acc_ref,
    first_hbm,
    second_hbm,
    lift_hbm,
    press_hbm,
    head_ref,
    label_ref,
    new_tables_ref,
    new_acc_ref,
    grad_first_ref,
    grad_second_ref,
    grad_lift_ref,
    grad_press_ref,
    logits_ref,
    w1h,
    w1l,
    w2f,
    w2h,
    w2l,
    lift,
    press,
    decayed,
    cols,
    feats,
    hidden,
    act,
    stats,
    rs_buf,
    gath,
    gl,
    gp,
    gsec,
    gt,
    load_sem,
    ag_send,
    ag_recv,
    rs_send,
    rs_recv,
    gm_send,
    gm_recv,
    gt_send,
    gt_recv,
):
    n, nt = dims
    me = lax.axis_index("member")
    tpos = lax.axis_index("tower")
    towers, bags, total = bag_ref.shape
    rows, width = tables_ref.shape[1:]
    hid, outs = w2f.shape[1:]
    fin = w1h.shape[1]
    rank = lift.shape[1]
    flat = towers * outs
    own = total // n
    piece = own // nt
    chunk = min(256, total)
    chips = n // 2
    chip, core = me // 2, lax.rem(me, 2)

    loads = []
    for t in range(towers):
        loads.append(pltpu.make_async_copy(first_hbm.at[t], hidden.at[t, :fin], load_sem.at[len(loads)]))
        loads.append(pltpu.make_async_copy(second_hbm.at[t], w2f.at[t], load_sem.at[len(loads)]))
    loads.append(
        pltpu.make_async_copy(lift_hbm.at[pl.ds(tpos * flat, flat)], lift, load_sem.at[len(loads)])
    )
    loads.append(
        pltpu.make_async_copy(press_hbm.at[pl.ds(tpos * flat, flat)], press, load_sem.at[len(loads)])
    )
    for load in loads:
        load.start()

    barrier = pltpu.get_barrier_semaphore()
    for d in range(1, n):
        pl.semaphore_signal(
            barrier, inc=1, device_id={"member": lax.rem(me + d, n)}, device_id_type=MESH
        )
    for d in range(1, nt):
        pl.semaphore_signal(
            barrier, inc=1, device_id={"tower": lax.rem(tpos + d, nt)}, device_id_type=MESH
        )

    stack = [bag_ref[t].astype(F32) for t in range(towers)]
    used = towers * bags
    stack.append(jnp.zeros((128 - used, total), F32))
    cols[...] = jnp.concatenate(stack, axis=0).T

    for t in range(towers):
        rates = jnp.exp(elapsed_ref[t : t + 1, :].astype(F32) * math.log(DECAY_RATE))
        ids = touch_ref[t : t + 1, :]
        place = lax.broadcasted_iota(jnp.int32, (rows, ids.shape[1]), 0)
        chosen = jnp.sum(jnp.where(place == ids, rates, 0.0), axis=1, keepdims=True)
        decayed[t] = tables_ref[t] * jnp.where(chosen > 0.0, chosen, 1.0)
    pairs = [jnp.concatenate(split(decayed[t]), axis=1) for t in range(towers)]
    for c in range(total // chunk):
        span = pl.ds(c * chunk, chunk)
        place = lax.broadcasted_iota(jnp.int32, (chunk, rows), 1).astype(F32)
        pooled = []
        for t in range(towers):
            counts = jnp.zeros((chunk, rows), F32)
            for b in range(bags):
                k = t * bags + b
                counts = counts + jnp.where(place == cols[span, k : k + 1], 1.0, 0.0)
            both = dot1(counts.astype(BF16), pairs[t])
            pooled.append(both[:, :width] + both[:, width:])
        feats[me, span, :] = jnp.concatenate(pooled, axis=1)

    pl.semaphore_wait(barrier, n - 1 + nt - 1)

    def block_copy(block, lane, target):
        return pltpu.make_async_remote_copy(
            src_ref=feats.at[block],
            dst_ref=feats.at[block],
            send_sem=ag_send.at[lane, block],
            recv_sem=ag_recv.at[block],
            device_id={"member": target},
            device_id_type=MESH,
        )

    def pass_on(block, right, left):
        if right:

            @pl.when(chip + 1 < chips)
            def _():
                block_copy(block, 0, me + 2).start()

        if left:

            @pl.when(chip > 0)
            def _():
                block_copy(block, 1, me - 2).start()

        block_copy(block, 2, me + 1 - 2 * core).start()

    def sent(block, right, left):
        if right:

            @pl.when(chip + 1 < chips)
            def _():
                block_copy(block, 0, me + 2).wait_send()

        if left:

            @pl.when(chip > 0)
            def _():
                block_copy(block, 1, me - 2).wait_send()

        block_copy(block, 2, me + 1 - 2 * core).wait_send()

    pass_on(me, True, True)

    for load in loads:
        load.wait()
    for t in range(towers):

        @pl.loop(0, fin // 64)
        def _(i):
            span = pl.ds(pl.multiple_of(i * 64, 64), 64)
            w1h[t, span, :], w1l[t, span, :] = split(hidden[t, span, :])

        @pl.loop(0, hid // 128)
        def _(i):
            span = pl.ds(pl.multiple_of(i * 128, 128), 128)
            w2h[t, span, :], w2l[t, span, :] = split(w2f[t, span, :])

    for d in range(1, chips):

        @pl.when(chip >= d)
        def _():
            block = me - 2 * d
            block_copy(block, 0, me).wait_recv()
            pass_on(block, True, False)

        @pl.when(chip + d < chips)
        def _():
            block = me + 2 * d
            block_copy(block, 0, me).wait_recv()
            pass_on(block, False, True)

    for c in range(chips):
        block_copy(2 * c + 1 - core, 0, me).wait_recv()

    sent(me, True, True)
    for d in range(1, chips):

        @pl.when(chip >= d)
        def _():
            sent(me - 2 * d, True, False)

        @pl.when(chip + d < chips)
        def _():
            sent(me + 2 * d, False, True)

    def features_of(t, span):
        return jnp.concatenate(
            [feats[j, span, t * width : (t + 1) * width] for j in range(n)], axis=1
        )

    head = head_ref[:, pl.ds(pl.multiple_of(tpos * flat, flat), flat)]
    lift_pair = split(lift[...])
    press_pair = split(press[...])

    mine = pl.ds(pl.multiple_of(me * own, own), own)
    flat_out = []
    for t in range(towers):
        h = dot3(split(features_of(t, mine)), (w1h[t], w1l[t]))
        flat_out.append(dot3(split(h * sigmoid(h)), (w2h[t], w2l[t])))
    flat_out = jnp.concatenate(flat_out, axis=1)
    weighted = flat_out * head
    stats[:, :rank] = dot3(split(flat_out), press_pair)
    stats[:, rank : 2 * rank] = dot3(split(weighted), lift_pair)
    stats[:, 2 * rank :] = jnp.broadcast_to(
        jnp.sum(weighted, axis=1, keepdims=True), (own, rank)
    )

    def tower_copy(d, reverse=False):
        other = lax.rem(tpos + d, nt)
        return pltpu.make_async_remote_copy(
            src_ref=stats.at[pl.ds(pl.multiple_of(other * piece, piece), piece)],
            dst_ref=rs_buf.at[tpos],
            send_sem=rs_send.at[d],
            recv_sem=rs_recv.at[d],
            device_id={"tower": other},
            device_id_type=MESH,
        )

    for d in range(1, nt):
        tower_copy(d).start()

    @pl.loop(0, total // chunk)
    def _(c):
        span = pl.ds(pl.multiple_of(c * chunk, chunk), chunk)
        for t in range(towers):
            hidden[t, span, :] = dot3(split(features_of(t, span)), (w1h[t], w1l[t]))

    for d in range(1, nt):
        tower_copy(d).wait_recv()
    summed = stats[pl.ds(pl.multiple_of(tpos * piece, piece), piece), :]
    for d in range(1, nt):
        summed = summed + rs_buf[lax.rem(tpos + d, nt)]
    logit = (
        jnp.sum(summed[:, :rank] * summed[:, rank : 2 * rank], axis=1, keepdims=True)
        + summed[:, 2 * rank :]
    )
    logits_ref[...] = logit
    error = sigmoid(logit) - label_ref[...]
    gath[me, tpos, :, :rank] = error * summed[:, :rank]
    gath[me, tpos, :, rank : 2 * rank] = error * summed[:, rank : 2 * rank]
    gath[me, tpos, :, 2 * rank :] = error
    for d in range(1, nt):
        tower_copy(d).wait_send()

    def member_copy(d):
        return pltpu.make_async_remote_copy(
            src_ref=gath.at[me, tpos],
            dst_ref=gath.at[me, tpos],
            send_sem=gm_send.at[d],
            recv_sem=gm_recv.at[d],
            device_id={"member": lax.rem(me + d, n)},
            device_id_type=MESH,
        )

    for d in range(1, n):
        member_copy(d).start()
    for d in range(1, n):
        member_copy(d).wait_recv()

    def column_copy(d):
        return pltpu.make_async_remote_copy(
            src_ref=gath.at[:, tpos],
            dst_ref=gath.at[:, tpos],
            send_sem=gt_send.at[d],
            recv_sem=gt_recv.at[d],
            device_id={"tower": lax.rem(tpos + d, nt)},
            device_id_type=MESH,
        )

    for d in range(1, nt):
        column_copy(d).start()
    for d in range(1, nt):
        column_copy(d).wait_recv()
    for d in range(1, n):
        member_copy(d).wait_send()
    for d in range(1, nt):
        column_copy(d).wait_send()

    block_hid = hid // n
    window = max(block_hid, 128)
    start = pl.multiple_of((me * block_hid) // 128 * 128, 128)
    grad_first_ref[...] = jnp.zeros_like(grad_first_ref)
    gsec[...] = jnp.zeros_like(gsec)
    gl[...] = jnp.zeros_like(gl)
    gp[...] = jnp.zeros_like(gp)
    gt[...] = jnp.zeros_like(gt)
    own_rows = pl.ds(pl.multiple_of(me * width, width), width)
    members_here = chunk // own

    for t in range(towers):

        @pl.loop(0, total // chunk)
        def _(c):
            span = pl.ds(pl.multiple_of(c * chunk, chunk), chunk)
            block = gath[pl.ds(c * members_here, members_here)].reshape(chunk, 3 * rank)
            ep = split(block[:, :rank])
            eg = split(block[:, rank : 2 * rank])
            part = slice(t * outs, (t + 1) * outs)
            head_t = head[:, part]
            lift_t = tuple(x[part] for x in lift_pair)
            press_t = tuple(x[part] for x in press_pair)
            w2 = (w2h[t], w2l[t])
            error_all = block[:, 2 * rank : 2 * rank + 1]
            grad_out = head_t * (error_all + dot3(ep, lift_t, NT)) + dot3(eg, press_t, NT)
            h = hidden[t, span, :]
            sig = sigmoid(h)
            a = h * sig
            act[...] = a
            tower_out = dot3(split(a), w2)
            gl[part] += dot3(split((tower_out * head_t).T), ep)
            gp[part] += dot3(split(tower_out.T), eg)
            go = split(grad_out)
            gsec[t] += dot3(split(act[:, pl.ds(start, window)].T), go)
            grad_hidden = split(dot3(go, w2, NT) * (sig * (1.0 + h * (1.0 - sig))))
            pooled = feats[me, span, :].T[t * width : (t + 1) * width]
            grad_first_ref[t] += dot3(split(pooled), grad_hidden)
            grad_pooled = dot3(grad_hidden, (w1h[t, own_rows, :], w1l[t, own_rows, :]), NT)
            counts = jnp.zeros((rows, chunk), F32)
            place = lax.broadcasted_iota(jnp.int32, (rows, chunk), 0)
            for b in range(bags):
                counts = counts + jnp.where(place == bag_ref[t, b : b + 1, span], 1.0, 0.0)
            both = dot1(counts.astype(BF16), jnp.concatenate(split(grad_pooled), axis=1))
            gt[t] += both[:, :width] + both[:, width:]

        shift = pl.multiple_of(me * block_hid - start, min(block_hid, 128))
        grad_second_ref[t] = gsec[t, pl.ds(shift, block_hid), :]

    own_flat = pl.ds(pl.multiple_of(me * (flat // n), flat // n), flat // n)
    grad_lift_ref[...] = gl[own_flat]
    grad_press_ref[...] = gp[own_flat]
    squares = []
    for t in range(towers):
        g = gt[t]
        squares.append(jnp.mean(g * g, axis=1, keepdims=True))
    wide = jnp.concatenate(squares + [jnp.zeros((rows, 128 - towers), F32)], axis=1).T
    new_acc_ref[...] = acc_ref[...] + wide[:towers]
    back = jnp.concatenate([acc_ref[...], jnp.zeros((128 - towers, rows), F32)], axis=0).T
    for t in range(towers):
        value = back[:, t : t + 1] + squares[t]
        new_tables_ref[t] = decayed[t] - LEARN_RATE * gt[t] / (jnp.sqrt(value) + EPSILON)


def per_device(n, nt, *args):
    bag_ids, touch_ids, elapsed, tables, accumulator, first, second, lift, press, head, labels = args
    towers, _, bags, total = bag_ids.shape
    rows, width = tables.shape[2:]
    fin, _, hid = first.shape
    outs = second.shape[2]
    rank = lift.shape[1]
    flat = towers * outs
    own = total // n
    piece = own // nt
    window = max(hid // n, 128)
    tpos = lax.axis_index("tower")
    label = lax.dynamic_slice_in_dim(labels[0], tpos * piece, piece, 0).astype(F32)
    label = jnp.broadcast_to(label[:, None], (piece, rank))
    vmem = pl.BlockSpec(memory_space=pltpu.VMEM)
    anys = pl.BlockSpec(memory_space=pl.ANY)
    chunk = min(256, total)
    sem = pltpu.SemaphoreType.DMA
    out = pl.pallas_call(
        functools.partial(kernel, (n, nt)),
        out_shape=(
            jax.ShapeDtypeStruct((towers, rows, width), F32),
            jax.ShapeDtypeStruct((towers, rows), F32),
            jax.ShapeDtypeStruct((towers, fin // n, hid), F32),
            jax.ShapeDtypeStruct((towers, hid // n, outs), F32),
            jax.ShapeDtypeStruct((flat // n, rank), F32),
            jax.ShapeDtypeStruct((flat // n, rank), F32),
            jax.ShapeDtypeStruct((piece, rank), F32),
        ),
        in_specs=[vmem] * 5 + [anys] * 4 + [vmem] * 2,
        out_specs=[vmem] * 7,
        scratch_shapes=[
            pltpu.VMEM((towers, fin, hid), BF16),
            pltpu.VMEM((towers, fin, hid), BF16),
            pltpu.VMEM((towers, hid, outs), F32),
            pltpu.VMEM((towers, hid, outs), BF16),
            pltpu.VMEM((towers, hid, outs), BF16),
            pltpu.VMEM((flat, rank), F32),
            pltpu.VMEM((flat, rank), F32),
            pltpu.VMEM((towers, rows, width), F32),
            pltpu.VMEM((total, 128), F32),
            pltpu.VMEM((n, total, towers * width), F32),
            pltpu.VMEM((towers, max(total, fin), hid), F32),
            pltpu.VMEM((chunk, hid), F32),
            pltpu.VMEM((own, 3 * rank), F32),
            pltpu.VMEM((nt, piece, 3 * rank), F32),
            pltpu.VMEM((n, nt, piece, 3 * rank), F32),
            pltpu.VMEM((flat, rank), F32),
            pltpu.VMEM((flat, rank), F32),
            pltpu.VMEM((towers, window, outs), F32),
            pltpu.VMEM((towers, rows, width), F32),
            sem((2 * towers + 2,)),
            sem((3, n)),
            sem((n,)),
            sem((nt,)),
            sem((nt,)),
            sem((n,)),
            sem((n,)),
            sem((nt,)),
            sem((nt,)),
        ],
        compiler_params=pltpu.CompilerParams(
            collective_id=0, has_side_effects=True, vmem_limit_bytes=67043328
        ),
    )(
        bag_ids[:, 0],
        touch_ids[:, 0],
        elapsed[:, 0],
        tables[:, 0],
        accumulator[:, 0],
        jnp.transpose(first, (1, 0, 2)),
        jnp.transpose(second, (1, 0, 2)),
        lift,
        press,
        head[None, :],
        label,
    )
    new_tables, new_acc, grad_first, grad_second, grad_lift, grad_press, logits = out
    return (
        new_tables[:, None],
        new_acc[:, None],
        jnp.transpose(grad_first, (1, 0, 2)),
        jnp.transpose(grad_second, (1, 0, 2)),
        grad_lift,
        grad_press,
        logits[:, 0][None, :],
    )


def solution(mesh):
    placed = (
        P("tower", "member", None, None),
        P("tower", "member", None),
        P("tower", "member", None),
        P("tower", "member", None, None),
        P("tower", "member", None),
        P(None, "tower", None),
        P(None, "tower", None),
        P(),
        P(),
        P(),
        P("member", None),
    )
    return jax.shard_map(
        functools.partial(per_device, mesh.shape["member"], mesh.shape["tower"]),
        mesh=mesh,
        in_specs=placed,
        out_specs=(
            P("tower", "member", None, None),
            P("tower", "member", None),
            P("member", "tower", None),
            P("member", "tower", None),
            P(("tower", "member"), None),
            P(("tower", "member"), None),
            P("member", "tower"),
        ),
        check_vma=False,
    )
```

time: 264 us -> 92.7 us (0.35)
  waiting for transfers between devices: 131 us -> 0 us
  Pallas kernels: 0 us -> 69.1 us
  blocking collectives: 39.6 us -> 0 us
  matrix products: 37 us -> 0 us
  between operations: 14.7 us -> 0.65 us
  starting transfers between devices: 10.1 us -> 0 us
  other arithmetic: 7.83 us -> 0.73 us
    unnamed x5 -> x0, waiting for transfers between devices: 76.8 us -> none
    pallas_call x0 -> x1, Pallas kernels: none -> 69.1 us  [per_device(): pl.pallas_call(functools.partial(kernel, (n, nt)), out_shape=(jax.ShapeDt...]
    psum x3 -> x0, blocking collectives: 39.6 us -> none  [the longest x1 16.3 us: per_device(): lax.psum(jnp.dot(flat_out, press_local, precision=PRECISE), 'tower')]
    dot_general x15 -> x0, matrix products: 37 us -> none  [the longest x1 7.1 us: per_device(): jnp.einsum('sth,ith->sti', grad_hidden, first_weight, precision=PRECISE)]
    reduce_scatter x1 -> x0, waiting for transfers between devices: 36.6 us -> none  [per_device(): lax.psum_scatter(jnp.einsum('sth,sto->hto', piece, grad_out, precision=PR...]
    all_to_all x2 -> x0, waiting for transfers between devices: 18 us -> none  [the longest x1 9.06 us: per_device(): lax.all_to_all(grad_features, 'member', split_axis=2, concat_axis=0, tile...]
    all_to_all x2 -> x0, starting transfers between devices: 9.99 us -> none  [the longest x1 6.35 us: per_device(): lax.all_to_all(pooled, 'member', split_axis=0, concat_axis=2, tiled=True)]
    unnamed x30 -> x12, local copies, waits for them, and re-layouts: 10.4 us -> 19.7 us
  transfers between devices with their start and end apart: 5 -> 0, of which waited for: 4 -> 0; matrix products, arithmetic and copies ran while one was open for 15% -> 0% of each run, Pallas kernels for 0% -> 0%
where the time goes in v1:
time: 92.7 us; the launch traced here: 92.2 us
  Pallas kernels  69.1 us (75%)
  local copies, waits for them, and re-layouts  21.7 us (23%)
    pallas_call x1, Pallas kernels, per_device(): pl.pallas_call(functools.partial(kernel, (n, nt)), out_shape=(jax.ShapeDt...  69.1 us
    unnamed x12, local copies, waits for them, and re-layouts  19.7 us

profile of v1, /device:TPU:0, one launch (start us, length us, event | category | flops | bytes accessed | tf_op | source)
XLA Modules:
  0.0 92.2 jit_solution(9768586661106497585)
XLA Ops:
  0.6 0.7 convert_bitcast_fusion
  1.4 1.3 %copy.38 = f32[2,1,512]{2,0,1:T(2,128)} copy(f32[2,1,512]{2,1,0:T(1,128)} %param.15) | data formatting | bytes 8192
  2.6 0.7 broadcast_in_dim.16.label_ref
  3.3 1.9 %copy.25 = f32[2,1,512,64]{3,2,0,1:T(8,128)} copy(f32[2,1,512,64]{2,3,1,0:T(8,128)} %param.14) | data formatting | bytes 524288 | tf_op args[3]
  5.3 0.0 copy-start
  5.3 3.2 %copy.37 = f32[1024,2,256]{2,0,1:T(8,128)} copy(f32[1024,2,256]{2,1,0:T(2,128)} %param.17) | data formatting | bytes 4194304 | tf_op args[6]
  8.5 0.0 copy-done
  8.5 3.2 %copy.36 = f32[512,2,1024]{2,0,1:T(8,128)} copy(f32[512,2,1024]{2,1,0:T(2,128)S(1)} %copy-done) | data formatting | bytes 8388608 | tf_op args[5]
  11.7 69.1 %shard_map.162 = (f32[2,512,64]{2,1,0:T(8,128)}, f32[2,512]{1,0:T(2,128)}, f32[2,64,1024]{2,1,0:T(8,128)}, f32[2,128,256]{2,1,0:T(8,128)}, f32[64,128]{1,0:T(8,1...) custom-call(s32[2,4,512]{2,1,0:T(4,128)} %bitcast.27, s32[2,128]{1,0:T(2,128)} %bitcast.31, s32[2,128]{1,0:T(2,128)} %bitcast.32, ...), custom_call_target="tpu_custom_call" | custom-call | tf_op jit(solution)/shard_map/pallas_call | solution.py:412
  80.8 1.9 %copy.28 = f32[2,1,512,64]{2,3,1,0:T(8,128)} copy(f32[2,1,512,64]{3,2,0,1:T(8,128)} %bitcast.24) | data formatting | bytes 524288
  82.7 1.3 %copy.29 = f32[2,1,512]{2,1,0:T(1,128)} copy(f32[2,1,512]{2,0,1:T(2,128)} %bitcast.30) | data formatting | bytes 8192
  84.0 1.3 %slice_reduce_fusion = f32[16]{0:T(128)} fusion(f32[16,128]{1,0:T(8,128)} %get-tuple-element.20), kind=kLoop, calls=%fused_computation.2 | loop fusion | bytes 128 | tf_op jit(solution)/shard_map/slice | solution.py:479
  85.3 1.9 %copy.31 = f32[128,2,256]{2,1,0:T(2,128)} copy(f32[128,2,256]{2,0,1:T(8,128)} %bitcast.26) | data formatting | bytes 524288
  87.2 2.2 %copy.30 = f32[64,2,1024]{2,1,0:T(2,128)} copy(f32[64,2,1024]{2,0,1:T(8,128)} %bitcast.25) | data formatting | bytes 1048576
  89.4 1.4 %copy.41 = f32[64,128]{1,0:T(8,128)} copy(f32[64,128]{1,0:T(8,128)} %get-tuple-element.46) | data formatting | bytes 65536
  90.8 1.4 %copy.42 = f32[64,128]{1,0:T(8,128)} copy(f32[64,128]{1,0:T(8,128)} %get-tuple-element.47) | data formatting | bytes 65536
Async XLA Ops:
  5.3 3.2 %copy-start = (f32[512,2,1024]{2,1,0:T(2,128)S(1)}, f32[512,2,1024]{2,1,0:T(2,128)}, u32[]{:S(2)}) copy-start(f32[512,2,1024]{2,1,0:T(2,128)} %param.16) | copy-start | bytes 12582916

commit v2 on v1

--- a/solution.py
+++ b/solution.py
@@ -36,26 +36,26 @@
     return 1.0 / (1.0 + jnp.exp(-x))
 
 
-def kernel(
+def gather_kernel(
     dims,
     bag_ref,
     touch_ref,
     elapsed_ref,
     tables_ref,
-    acc_ref,
     first_hbm,
     second_hbm,
     lift_hbm,
     press_hbm,
     head_ref,
     label_ref,
-    new_tables_ref,
-    new_acc_ref,
-    grad_first_ref,
-    grad_second_ref,
-    grad_lift_ref,
-    grad_press_ref,
     logits_ref,
+    decayed_ref,
+    pooled_out,
+    hidden_out,
+    gath_out,
+    counts_out,
+    w2h_out,
+    w2l_out,
     w1h,
     w1l,
     w2f,
@@ -63,19 +63,16 @@
     w2l,
     lift,
     press,
-    decayed,
     cols,
+    counts_ref,
     feats,
     hidden,
-    act,
     stats,
     rs_buf,
     gath,
-    gl,
-    gp,
-    gsec,
-    gt,
     load_sem,
+    store_sem,
+    hidden_sem,
     ag_send,
     ag_recv,
     rs_send,
@@ -89,8 +86,9 @@
     me = lax.axis_index("member")
     tpos = lax.axis_index("tower")
     towers, bags, total = bag_ref.shape
-    rows, width = tables_ref.shape[1:]
-    hid, outs = w2f.shape[1:]
+    width, rows = tables_ref.shape[1:]
+    touches = touch_ref.shape[2]
+    hid, outs = w2h.shape[1:]
     fin = w1h.shape[1]
     rank = lift.shape[1]
     flat = towers * outs
@@ -101,17 +99,16 @@
     chip, core = me // 2, lax.rem(me, 2)
 
     loads = []
+
+    def load(source, target):
+        loads.append(pltpu.make_async_copy(source, target, load_sem.at[len(loads)]))
+        loads[-1].start()
+
     for t in range(towers):
-        loads.append(pltpu.make_async_copy(first_hbm.at[t], hidden.at[t, :fin], load_sem.at[len(loads)]))
-        loads.append(pltpu.make_async_copy(second_hbm.at[t], w2f.at[t], load_sem.at[len(loads)]))
-    loads.append(
-        pltpu.make_async_copy(lift_hbm.at[pl.ds(tpos * flat, flat)], lift, load_sem.at[len(loads)])
-    )
-    loads.append(
-        pltpu.make_async_copy(press_hbm.at[pl.ds(tpos * flat, flat)], press, load_sem.at[len(loads)])
-    )
-    for load in loads:
-        load.start()
+        load(first_hbm.at[:, t, :], hidden.at[t, :fin])
+        load(second_hbm.at[:, t, :], w2f.at[t])
+    load(lift_hbm.at[pl.ds(tpos * flat, flat)], lift)
+    load(press_hbm.at[pl.ds(tpos * flat, flat)], press)
 
     barrier = pltpu.get_barrier_semaphore()
     for d in range(1, n):
@@ -124,17 +121,22 @@
         )
 
     stack = [bag_ref[t].astype(F32) for t in range(towers)]
-    used = towers * bags
-    stack.append(jnp.zeros((128 - used, total), F32))
+    stack.append(jnp.zeros((128 - towers * bags, total), F32))
     cols[...] = jnp.concatenate(stack, axis=0).T
-
+    stack = []
     for t in range(towers):
-        rates = jnp.exp(elapsed_ref[t : t + 1, :].astype(F32) * math.log(DECAY_RATE))
-        ids = touch_ref[t : t + 1, :]
-        place = lax.broadcasted_iota(jnp.int32, (rows, ids.shape[1]), 0)
-        chosen = jnp.sum(jnp.where(place == ids, rates, 0.0), axis=1, keepdims=True)
-        decayed[t] = tables_ref[t] * jnp.where(chosen > 0.0, chosen, 1.0)
-    pairs = [jnp.concatenate(split(decayed[t]), axis=1) for t in range(towers)]
+        stack.append(touch_ref[t].astype(F32))
+        stack.append(jnp.exp(elapsed_ref[t].astype(F32) * math.log(DECAY_RATE)))
+    stack.append(jnp.zeros((128 - 2 * towers, touches), F32))
+    owed = jnp.concatenate(stack, axis=0).T
+    pairs = []
+    place = lax.broadcasted_iota(jnp.int32, (touches, rows), 1).astype(F32)
+    for t in range(towers):
+        ids, rates = owed[:, 2 * t : 2 * t + 1], owed[:, 2 * t + 1 : 2 * t + 2]
+        chosen = jnp.sum(jnp.where(place == ids, rates, 0.0), axis=0, keepdims=True)
+        decayed = tables_ref[t] * jnp.where(chosen > 0.0, chosen, 1.0)
+        decayed_ref[t] = decayed
+        pairs.append(jnp.concatenate(split(decayed), axis=0))
     for c in range(total // chunk):
         span = pl.ds(c * chunk, chunk)
         place = lax.broadcasted_iota(jnp.int32, (chunk, rows), 1).astype(F32)
@@ -144,7 +146,9 @@
             for b in range(bags):
                 k = t * bags + b
                 counts = counts + jnp.where(place == cols[span, k : k + 1], 1.0, 0.0)
-            both = dot1(counts.astype(BF16), pairs[t])
+            counts = counts.astype(BF16)
+            counts_ref[t, span, :] = counts
+            both = dot1(counts, pairs[t], NT)
             pooled.append(both[:, :width] + both[:, width:])
         feats[me, span, :] = jnp.concatenate(pooled, axis=1)
 
@@ -192,8 +196,16 @@
 
     pass_on(me, True, True)
 
-    for load in loads:
-        load.wait()
+    stores = []
+
+    def store(source, target):
+        stores.append(pltpu.make_async_copy(source, target, store_sem.at[len(stores)]))
+        stores[-1].start()
+
+    store(counts_ref, counts_out)
+
+    for copy in loads:
+        copy.wait()
     for t in range(towers):
 
         @pl.loop(0, fin // 64)
@@ -205,6 +217,10 @@
         def _(i):
             span = pl.ds(pl.multiple_of(i * 128, 128), 128)
             w2h[t, span, :], w2l[t, span, :] = split(w2f[t, span, :])
+
+    store(w2h, w2h_out)
+    store(w2l, w2l_out)
+    store(feats.at[me], pooled_out)
 
     for d in range(1, chips):
 
@@ -223,25 +239,12 @@
     for c in range(chips):
         block_copy(2 * c + 1 - core, 0, me).wait_recv()
 
-    sent(me, True, True)
-    for d in range(1, chips):
-
-        @pl.when(chip >= d)
-        def _():
-            sent(me - 2 * d, True, False)
-
-        @pl.when(chip + d < chips)
-        def _():
-            sent(me + 2 * d, False, True)
-
     def features_of(t, span):
         return jnp.concatenate(
             [feats[j, span, t * width : (t + 1) * width] for j in range(n)], axis=1
         )
 
     head = head_ref[:, pl.ds(pl.multiple_of(tpos * flat, flat), flat)]
-    lift_pair = split(lift[...])
-    press_pair = split(press[...])
 
     mine = pl.ds(pl.multiple_of(me * own, own), own)
     flat_out = []
@@ -250,13 +253,13 @@
         flat_out.append(dot3(split(h * sigmoid(h)), (w2h[t], w2l[t])))
     flat_out = jnp.concatenate(flat_out, axis=1)
     weighted = flat_out * head
-    stats[:, :rank] = dot3(split(flat_out), press_pair)
-    stats[:, rank : 2 * rank] = dot3(split(weighted), lift_pair)
+    stats[:, :rank] = dot3(split(flat_out), split(press[...]))
+    stats[:, rank : 2 * rank] = dot3(split(weighted), split(lift[...]))
     stats[:, 2 * rank :] = jnp.broadcast_to(
         jnp.sum(weighted, axis=1, keepdims=True), (own, rank)
     )
 
-    def tower_copy(d, reverse=False):
+    def tower_copy(d):
         other = lax.rem(tpos + d, nt)
         return pltpu.make_async_remote_copy(
             src_ref=stats.at[pl.ds(pl.multiple_of(other * piece, piece), piece)],
@@ -270,11 +273,19 @@
     for d in range(1, nt):
         tower_copy(d).start()
 
-    @pl.loop(0, total // chunk)
-    def _(c):
+    def hidden_copy(t, c):
+        span = pl.ds(pl.multiple_of(c * chunk, chunk), chunk)
+        return pltpu.make_async_copy(
+            hidden.at[t, span], hidden_out.at[t, span], hidden_sem.at[t, c]
+        )
+
+    def hidden_chunk(c):
         span = pl.ds(pl.multiple_of(c * chunk, chunk), chunk)
         for t in range(towers):
             hidden[t, span, :] = dot3(split(features_of(t, span)), (w1h[t], w1l[t]))
+            hidden_copy(t, c).start()
+
+    pl.loop(0, total // chunk)(hidden_chunk)
 
     for d in range(1, nt):
         tower_copy(d).wait_recv()
@@ -290,8 +301,6 @@
     gath[me, tpos, :, :rank] = error * summed[:, :rank]
     gath[me, tpos, :, rank : 2 * rank] = error * summed[:, rank : 2 * rank]
     gath[me, tpos, :, 2 * rank :] = error
-    for d in range(1, nt):
-        tower_copy(d).wait_send()
 
     def member_copy(d):
         return pltpu.make_async_remote_copy(
@@ -305,6 +314,19 @@
 
     for d in range(1, n):
         member_copy(d).start()
+    for d in range(1, nt):
+        tower_copy(d).wait_send()
+    sent(me, True, True)
+    for d in range(1, chips):
+
+        @pl.when(chip >= d)
+        def _():
+            sent(me - 2 * d, True, False)
+
+        @pl.when(chip + d < chips)
+        def _():
+            sent(me + 2 * d, False, True)
+
     for d in range(1, n):
         member_copy(d).wait_recv()
 
@@ -322,35 +344,120 @@
         column_copy(d).start()
     for d in range(1, nt):
         column_copy(d).wait_recv()
+    store(gath, gath_out)
     for d in range(1, n):
         member_copy(d).wait_send()
     for d in range(1, nt):
         column_copy(d).wait_send()
+
+    @pl.loop(0, total // chunk)
+    def _(c):
+        for t in range(towers):
+            hidden_copy(t, c).wait()
+
+    for copy in stores:
+        copy.wait()
+
+
+def update_kernel(
+    dims,
+    acc_ref,
+    decayed_ref,
+    first_ref,
+    pooled_ref,
+    gath_ref,
+    w2h_ref,
+    w2l_ref,
+    lift_hbm,
+    press_hbm,
+    head_ref,
+    hidden_hbm,
+    counts_hbm,
+    new_tables_ref,
+    new_acc_ref,
+    grad_first_ref,
+    grad_second_ref,
+    grad_lift_ref,
+    grad_press_ref,
+    lift,
+    press,
+    hidden,
+    counts,
+    act,
+    gl,
+    gp,
+    gf,
+    gsec,
+    gt,
+    load_sem,
+    hidden_sem,
+    counts_sem,
+):
+    n, nt = dims
+    me = lax.axis_index("member")
+    tpos = lax.axis_index("tower")
+    towers, total, hid = hidden.shape
+    width, rows = decayed_ref.shape[1:]
+    outs = w2h_ref.shape[2]
+    rank = lift.shape[1]
+    flat = towers * outs
+    own = total // n
+    chunk = min(256, total)
+
+    loads = []
+
+    def load(source, target):
+        loads.append(pltpu.make_async_copy(source, target, load_sem.at[len(loads)]))
+        loads[-1].start()
+
+    load(lift_hbm.at[pl.ds(tpos * flat, flat)], lift)
+    load(press_hbm.at[pl.ds(tpos * flat, flat)], press)
+
+    def hidden_copy(t, c):
+        span = pl.ds(pl.multiple_of(c * chunk, chunk), chunk)
+        return pltpu.make_async_copy(
+            hidden_hbm.at[t, span], hidden.at[t, span], hidden_sem.at[t, c]
+        )
+
+    def counts_copy(t):
+        return pltpu.make_async_copy(counts_hbm.at[t], counts.at[t], counts_sem.at[t])
+
+    for t in range(towers):
+        for c in range(total // chunk):
+            hidden_copy(t, c).start()
+        counts_copy(t).start()
 
     block_hid = hid // n
     window = max(block_hid, 128)
     start = pl.multiple_of((me * block_hid) // 128 * 128, 128)
-    grad_first_ref[...] = jnp.zeros_like(grad_first_ref)
+    gf[...] = jnp.zeros_like(gf)
     gsec[...] = jnp.zeros_like(gsec)
     gl[...] = jnp.zeros_like(gl)
     gp[...] = jnp.zeros_like(gp)
     gt[...] = jnp.zeros_like(gt)
-    own_rows = pl.ds(pl.multiple_of(me * width, width), width)
     members_here = chunk // own
+    head = head_ref[:, pl.ds(pl.multiple_of(tpos * flat, flat), flat)]
+    for copy in loads:
+        copy.wait()
+    lift_pair = split(lift[...])
+    press_pair = split(press[...])
 
     for t in range(towers):
+        counts_copy(t).wait()
+        first = split(first_ref[:, t, :])
 
         @pl.loop(0, total // chunk)
         def _(c):
+            hidden_copy(t, c).wait()
             span = pl.ds(pl.multiple_of(c * chunk, chunk), chunk)
-            block = gath[pl.ds(c * members_here, members_here)].reshape(chunk, 3 * rank)
+            block = gath_ref[pl.ds(c * members_here, members_here)].reshape(chunk, 3 * rank)
             ep = split(block[:, :rank])
             eg = split(block[:, rank : 2 * rank])
             part = slice(t * outs, (t + 1) * outs)
             head_t = head[:, part]
             lift_t = tuple(x[part] for x in lift_pair)
             press_t = tuple(x[part] for x in press_pair)
-            w2 = (w2h[t], w2l[t])
+            w2 = (w2h_ref[t], w2l_ref[t])
             error_all = block[:, 2 * rank : 2 * rank + 1]
             grad_out = head_t * (error_all + dot3(ep, lift_t, NT)) + dot3(eg, press_t, NT)
             h = hidden[t, span, :]
@@ -363,32 +470,23 @@
             go = split(grad_out)
             gsec[t] += dot3(split(act[:, pl.ds(start, window)].T), go)
             grad_hidden = split(dot3(go, w2, NT) * (sig * (1.0 + h * (1.0 - sig))))
-            pooled = feats[me, span, :].T[t * width : (t + 1) * width]
-            grad_first_ref[t] += dot3(split(pooled), grad_hidden)
-            grad_pooled = dot3(grad_hidden, (w1h[t, own_rows, :], w1l[t, own_rows, :]), NT)
-            counts = jnp.zeros((rows, chunk), F32)
-            place = lax.broadcasted_iota(jnp.int32, (rows, chunk), 0)
-            for b in range(bags):
-                counts = counts + jnp.where(place == bag_ref[t, b : b + 1, span], 1.0, 0.0)
-            both = dot1(counts.astype(BF16), jnp.concatenate(split(grad_pooled), axis=1))
-            gt[t] += both[:, :width] + both[:, width:]
+            pooled = pooled_ref[span, :].T[t * width : (t + 1) * width]
+            gf[t] += dot3(split(pooled), grad_hidden)
+            grad_pooled = dot3(first, grad_hidden, NT)
+            both = dot1(jnp.concatenate(split(grad_pooled), axis=0), counts[t, span, :])
+            gt[t] += both[:width] + both[width:]
 
         shift = pl.multiple_of(me * block_hid - start, min(block_hid, 128))
-        grad_second_ref[t] = gsec[t, pl.ds(shift, block_hid), :]
+        grad_second_ref[:, t, :] = gsec[t, pl.ds(shift, block_hid), :]
+        grad_first_ref[:, t, :] = gf[t]
+        g = gt[t]
+        value = acc_ref[t] + jnp.mean(g * g, axis=0, keepdims=True)
+        new_acc_ref[t] = value
+        new_tables_ref[t] = decayed_ref[t] - LEARN_RATE * g / (jnp.sqrt(value) + EPSILON)
 
     own_flat = pl.ds(pl.multiple_of(me * (flat // n), flat // n), flat // n)
     grad_lift_ref[...] = gl[own_flat]
     grad_press_ref[...] = gp[own_flat]
-    squares = []
-    for t in range(towers):
-        g = gt[t]
-        squares.append(jnp.mean(g * g, axis=1, keepdims=True))
-    wide = jnp.concatenate(squares + [jnp.zeros((rows, 128 - towers), F32)], axis=1).T
-    new_acc_ref[...] = acc_ref[...] + wide[:towers]
-    back = jnp.concatenate([acc_ref[...], jnp.zeros((128 - towers, rows), F32)], axis=0).T
-    for t in range(towers):
-        value = back[:, t : t + 1] + squares[t]
-        new_tables_ref[t] = decayed[t] - LEARN_RATE * gt[t] / (jnp.sqrt(value) + EPSILON)
 
 
 def per_device(n, nt, *args):
@@ -401,7 +499,9 @@
     flat = towers * outs
     own = total // n
     piece = own // nt
-    window = max(hid // n, 128)
+    block_hid = hid // n
+    window = max(block_hid, 128)
+    me = lax.axis_index("member")
     tpos = lax.axis_index("tower")
     label = lax.dynamic_slice_in_dim(labels[0], tpos * piece, piece, 0).astype(F32)
     label = jnp.broadcast_to(label[:, None], (piece, rank))
@@ -409,19 +509,22 @@
     anys = pl.BlockSpec(memory_space=pl.ANY)
     chunk = min(256, total)
     sem = pltpu.SemaphoreType.DMA
-    out = pl.pallas_call(
-        functools.partial(kernel, (n, nt)),
+    lanes = towers * width
+    shape = jax.ShapeDtypeStruct
+    logits, decayed, pooled, hidden, gath, counts, w2h, w2l = pl.pallas_call(
+        functools.partial(gather_kernel, (n, nt)),
         out_shape=(
-            jax.ShapeDtypeStruct((towers, rows, width), F32),
-            jax.ShapeDtypeStruct((towers, rows), F32),
-            jax.ShapeDtypeStruct((towers, fin // n, hid), F32),
-            jax.ShapeDtypeStruct((towers, hid // n, outs), F32),
-            jax.ShapeDtypeStruct((flat // n, rank), F32),
-            jax.ShapeDtypeStruct((flat // n, rank), F32),
-            jax.ShapeDtypeStruct((piece, rank), F32),
+            shape((piece, rank), F32),
+            shape((towers, width, rows), F32),
+            shape((total, lanes), F32),
+            shape((towers, total, hid), F32),
+            shape((n, nt, piece, 3 * rank), F32),
+            shape((towers, total, rows), BF16),
+            shape((towers, hid, outs), BF16),
+            shape((towers, hid, outs), BF16),
         ),
-        in_specs=[vmem] * 5 + [anys] * 4 + [vmem] * 2,
-        out_specs=[vmem] * 7,
+        in_specs=[vmem] * 4 + [anys] * 4 + [vmem] * 2,
+        out_specs=[vmem] * 2 + [anys] * 6,
         scratch_shapes=[
             pltpu.VMEM((towers, fin, hid), BF16),
             pltpu.VMEM((towers, fin, hid), BF16),
@@ -430,19 +533,16 @@
             pltpu.VMEM((towers, hid, outs), BF16),
             pltpu.VMEM((flat, rank), F32),
             pltpu.VMEM((flat, rank), F32),
-            pltpu.VMEM((towers, rows, width), F32),
             pltpu.VMEM((total, 128), F32),
-            pltpu.VMEM((n, total, towers * width), F32),
+            pltpu.VMEM((towers, total, rows), BF16),
+            pltpu.VMEM((n, total, lanes), F32),
             pltpu.VMEM((towers, max(total, fin), hid), F32),
-            pltpu.VMEM((chunk, hid), F32),
             pltpu.VMEM((own, 3 * rank), F32),
             pltpu.VMEM((nt, piece, 3 * rank), F32),
             pltpu.VMEM((n, nt, piece, 3 * rank), F32),
-            pltpu.VMEM((flat, rank), F32),
-            pltpu.VMEM((flat, rank), F32),
-            pltpu.VMEM((towers, window, outs), F32),
-            pltpu.VMEM((towers, rows, width), F32),
             sem((2 * towers + 2,)),
+            sem((5,)),
+            sem((towers, total // chunk)),
             sem((3, n)),
             sem((n,)),
             sem((nt,)),
@@ -457,23 +557,70 @@
         ),
     )(
         bag_ids[:, 0],
-        touch_ids[:, 0],
-        elapsed[:, 0],
-        tables[:, 0],
-        accumulator[:, 0],
-        jnp.transpose(first, (1, 0, 2)),
-        jnp.transpose(second, (1, 0, 2)),
+        touch_ids,
+        elapsed,
+        jnp.transpose(tables[:, 0], (0, 2, 1)),
+        first,
+        second,
         lift,
         press,
         head[None, :],
         label,
     )
-    new_tables, new_acc, grad_first, grad_second, grad_lift, grad_press, logits = out
+    out = pl.pallas_call(
+        functools.partial(update_kernel, (n, nt)),
+        out_shape=(
+            shape((towers, width, rows), F32),
+            shape((towers, 1, rows), F32),
+            shape((width, towers, hid), F32),
+            shape((block_hid, towers, outs), F32),
+            shape((flat // n, rank), F32),
+            shape((flat // n, rank), F32),
+        ),
+        grid=(1,),
+        in_specs=[vmem] * 2
+        + [pl.BlockSpec((width, towers, hid), lambda i: (lax.axis_index("member"), 0, 0))]
+        + [vmem] * 4
+        + [anys] * 2
+        + [vmem]
+        + [anys] * 2,
+        out_specs=[vmem] * 6,
+        scratch_shapes=[
+            pltpu.VMEM((flat, rank), F32),
+            pltpu.VMEM((flat, rank), F32),
+            pltpu.VMEM((towers, total, hid), F32),
+            pltpu.VMEM((towers, total, rows), BF16),
+            pltpu.VMEM((chunk, hid), F32),
+            pltpu.VMEM((flat, rank), F32),
+            pltpu.VMEM((flat, rank), F32),
+            pltpu.VMEM((towers, width, hid), F32),
+            pltpu.VMEM((towers, window, outs), F32),
+            pltpu.VMEM((towers, width, rows), F32),
+            sem((2,)),
+            sem((towers, total // chunk)),
+            sem((towers,)),
+        ],
+        compiler_params=pltpu.CompilerParams(vmem_limit_bytes=67043328),
+    )(
+        accumulator,
+        decayed,
+        first,
+        pooled,
+        gath,
+        w2h,
+        w2l,
+        lift,
+        press,
+        head[None, :],
+        hidden,
+        counts,
+    )
+    new_tables, new_acc, grad_first, grad_second, grad_lift, grad_press = out
     return (
-        new_tables[:, None],
-        new_acc[:, None],
-        jnp.transpose(grad_first, (1, 0, 2)),
-        jnp.transpose(grad_second, (1, 0, 2)),
+        jnp.transpose(new_tables, (0, 2, 1))[:, None],
+        new_acc,
+        grad_first,
+        grad_second,
         grad_lift,
         grad_press,
         logits[:, 0][None, :],

time: 92.7 us -> 77.3 us (0.83)
  local copies, waits for them, and re-layouts: 21.7 us -> 1.99 us
  Pallas kernels: 69.1 us -> 73.7 us
    unnamed x12 -> x0, local copies, waits for them, and re-layouts: 19.7 us -> none
    pallas_call x1 -> x2, Pallas kernels: 69.1 us -> 73.7 us  [the longest x1 51.6 us: per_device(): pl.pallas_call(functools.partial(gather_kernel, (n, nt)), out_shape=(shap...]
where the time goes in v2:
time: 77.3 us; the launch traced here: 77.1 us
  Pallas kernels  73.7 us (95%)
  local copies, waits for them, and re-layouts  1.99 us (3%)
    pallas_call x1, Pallas kernels, per_device(): pl.pallas_call(functools.partial(gather_kernel, (n, nt)), out_shape=(shap...  51.6 us
    pallas_call x1, Pallas kernels, per_device(): pl.pallas_call(functools.partial(update_kernel, (n, nt)), out_shape=(shap...  22.2 us

profile of v2, /device:TPU:0, one launch (start us, length us, event | category | flops | bytes accessed | tf_op | source)
XLA Modules:
  0.0 77.1 jit_solution(10764467796566992688)
XLA Ops:
  0.6 0.7 convert_bitcast_fusion
  1.4 0.7 broadcast_in_dim.14.label_ref
  2.0 51.6 %shard_map.162 = (f32[16,128]{1,0:T(8,128)}, f32[2,64,512]{2,1,0:T(8,128)}, f32[512,128]{1,0:T(8,128)}, f32[2,512,1024]{2,1,0:T(8,128)}, f32[8,4,16,384]{3,2,1,0...) custom-call(s32[2,4,512]{2,1,0:T(4,128)} %bitcast.16, ...), custom_call_target="tpu_custom_call" | custom-call | tf_op jit(solution)/shard_map/pallas_call | solution.py:514
  53.6 22.2 %shard_map.163 = (f32[2,64,512]{2,1,0:T(8,128)}, f32[2,1,512]{2,1,0:T(1,128)}, f32[64,2,1024]{2,1,0:T(2,128)}, f32[128,2,256]{2,1,0:T(2,128)}, f32[64,128]{1,0:T(8,128)}, /*index=5*/f32[64,128]{1,0:T(8,128)}) custom-call(f32[2,1,512]{2,1,0:T(1,128)} %acc_ref.1, f32[2,64,512]{2,1,0:T(8,128)} %get-tuple-element.21.decayed_ref, f32[512,2,1024]{2,1,0:T(2,128)} %first_ref.1, ...), custom_call_target="tpu_custom_call" | custom-call | tf_op jit(solution)/shard_map/pallas_call | solution.py:570
  75.8 1.3 %slice_reduce_fusion = f32[16]{0:T(128)} fusion(f32[16,128]{1,0:T(8,128)} %get-tuple-element.34), kind=kLoop, calls=%fused_computation | loop fusion | bytes 128 | tf_op jit(solution)/shard_map/slice | solution.py:626

commit v3 on v2

--- a/solution.py
+++ b/solution.py
@@ -56,6 +56,7 @@
     counts_out,
     w2h_out,
     w2l_out,
+    tower_out_hbm,
     w1h,
     w1l,
     w2f,
@@ -67,6 +68,7 @@
     counts_ref,
     feats,
     hidden,
+    tower_out,
     stats,
     rs_buf,
     gath,
@@ -222,6 +224,24 @@
     store(w2l, w2l_out)
     store(feats.at[me], pooled_out)
 
+    def accumulate(source, fresh):
+        block_copy(2 * source + 1 - core, 0, me).wait_recv()
+        ins = pl.ds(pl.multiple_of(source * 2 * width, 2 * width), 2 * width)
+
+        @pl.loop(0, total // chunk)
+        def _(c):
+            span = pl.ds(pl.multiple_of(c * chunk, chunk), chunk)
+            even, odd = feats[2 * source, span, :], feats[2 * source + 1, span, :]
+            for t in range(towers):
+                part = slice(t * width, (t + 1) * width)
+                x = jnp.concatenate([even[:, part], odd[:, part]], axis=1)
+                h = dot3(split(x), (w1h[t, ins, :], w1l[t, ins, :]))
+                if fresh:
+                    hidden[t, span, :] = h
+                else:
+                    hidden[t, span, :] += h
+
+    accumulate(chip, True)
     for d in range(1, chips):
 
         @pl.when(chip >= d)
@@ -236,20 +256,26 @@
             block_copy(block, 0, me).wait_recv()
             pass_on(block, False, True)
 
-    for c in range(chips):
-        block_copy(2 * c + 1 - core, 0, me).wait_recv()
-
-    def features_of(t, span):
-        return jnp.concatenate(
-            [feats[j, span, t * width : (t + 1) * width] for j in range(n)], axis=1
-        )
+        @pl.when(chip >= d)
+        def _():
+            accumulate(chip - d, False)
+
+        @pl.when(chip + d < chips)
+        def _():
+            accumulate(chip + d, False)
+
+    def hidden_copy(t):
+        return pltpu.make_async_copy(hidden.at[t, :total], hidden_out.at[t], hidden_sem.at[t])
+
+    for t in range(towers):
+        hidden_copy(t).start()
 
     head = head_ref[:, pl.ds(pl.multiple_of(tpos * flat, flat), flat)]
 
     mine = pl.ds(pl.multiple_of(me * own, own), own)
     flat_out = []
     for t in range(towers):
-        h = dot3(split(features_of(t, mine)), (w1h[t], w1l[t]))
+        h = hidden[t, mine, :]
         flat_out.append(dot3(split(h * sigmoid(h)), (w2h[t], w2l[t])))
     flat_out = jnp.concatenate(flat_out, axis=1)
     weighted = flat_out * head
@@ -273,19 +299,16 @@
     for d in range(1, nt):
         tower_copy(d).start()
 
-    def hidden_copy(t, c):
-        span = pl.ds(pl.multiple_of(c * chunk, chunk), chunk)
-        return pltpu.make_async_copy(
-            hidden.at[t, span], hidden_out.at[t, span], hidden_sem.at[t, c]
-        )
-
-    def hidden_chunk(c):
-        span = pl.ds(pl.multiple_of(c * chunk, chunk), chunk)
-        for t in range(towers):
-            hidden[t, span, :] = dot3(split(features_of(t, span)), (w1h[t], w1l[t]))
-            hidden_copy(t, c).start()
-
-    pl.loop(0, total // chunk)(hidden_chunk)
+    def tower_chunks(t):
+        @pl.loop(0, total // chunk)
+        def _(c):
+            span = pl.ds(pl.multiple_of(c * chunk, chunk), chunk)
+            h = hidden[t, span, :]
+            tower_out[t, span, :] = dot3(split(h * sigmoid(h)), (w2h[t], w2l[t]))
+
+        store(tower_out.at[t], tower_out_hbm.at[t])
+
+    tower_chunks(0)
 
     for d in range(1, nt):
         tower_copy(d).wait_recv()
@@ -297,7 +320,10 @@
         + summed[:, 2 * rank :]
     )
     logits_ref[...] = logit
-    error = sigmoid(logit) - label_ref[...]
+    place = lax.broadcasted_iota(jnp.int32, (piece, own), 1)
+    wanted = lax.broadcasted_iota(jnp.int32, (piece, own), 0) + tpos * piece
+    clicks = jnp.where(place == wanted, label_ref[...].astype(F32), 0.0)
+    error = sigmoid(logit) - jnp.sum(clicks, axis=1, keepdims=True)
     gath[me, tpos, :, :rank] = error * summed[:, :rank]
     gath[me, tpos, :, rank : 2 * rank] = error * summed[:, rank : 2 * rank]
     gath[me, tpos, :, 2 * rank :] = error
@@ -314,6 +340,8 @@
 
     for d in range(1, n):
         member_copy(d).start()
+    for t in range(1, towers):
+        tower_chunks(t)
     for d in range(1, nt):
         tower_copy(d).wait_send()
     sent(me, True, True)
@@ -350,17 +378,16 @@
     for d in range(1, nt):
         column_copy(d).wait_send()
 
-    @pl.loop(0, total // chunk)
-    def _(c):
-        for t in range(towers):
-            hidden_copy(t, c).wait()
-
+    for t in range(towers):
+        hidden_copy(t).wait()
     for copy in stores:
         copy.wait()
 
 
 def update_kernel(
     dims,
+    logits_ref,
+    tower_out_ref,
     acc_ref,
     decayed_ref,
     first_ref,
@@ -379,6 +406,7 @@
     grad_second_ref,
     grad_lift_ref,
     grad_press_ref,
+    logits_out_ref,
     lift,
     press,
     hidden,
@@ -464,7 +492,7 @@
             sig = sigmoid(h)
             a = h * sig
             act[...] = a
-            tower_out = dot3(split(a), w2)
+            tower_out = tower_out_ref[t, span, :]
             gl[part] += dot3(split((tower_out * head_t).T), ep)
             gp[part] += dot3(split(tower_out.T), eg)
             go = split(grad_out)
@@ -487,6 +515,11 @@
     own_flat = pl.ds(pl.multiple_of(me * (flat // n), flat // n), flat // n)
     grad_lift_ref[...] = gl[own_flat]
     grad_press_ref[...] = gp[own_flat]
+    piece = logits_ref.shape[0]
+    place = lax.broadcasted_iota(jnp.int32, (piece, piece), 1)
+    wanted = lax.broadcasted_iota(jnp.int32, (piece, piece), 0)
+    values = jnp.where(place == wanted, logits_ref[:, :1], 0.0)
+    logits_out_ref[...] = jnp.sum(values, axis=0, keepdims=True)
 
 
 def per_device(n, nt, *args):
@@ -501,17 +534,13 @@
     piece = own // nt
     block_hid = hid // n
     window = max(block_hid, 128)
-    me = lax.axis_index("member")
-    tpos = lax.axis_index("tower")
-    label = lax.dynamic_slice_in_dim(labels[0], tpos * piece, piece, 0).astype(F32)
-    label = jnp.broadcast_to(label[:, None], (piece, rank))
     vmem = pl.BlockSpec(memory_space=pltpu.VMEM)
     anys = pl.BlockSpec(memory_space=pl.ANY)
     chunk = min(256, total)
     sem = pltpu.SemaphoreType.DMA
     lanes = towers * width
     shape = jax.ShapeDtypeStruct
-    logits, decayed, pooled, hidden, gath, counts, w2h, w2l = pl.pallas_call(
+    logits, decayed, pooled, hidden, gath, counts, w2h, w2l, tower_out = pl.pallas_call(
         functools.partial(gather_kernel, (n, nt)),
         out_shape=(
             shape((piece, rank), F32),
@@ -522,9 +551,10 @@
             shape((towers, total, rows), BF16),
             shape((towers, hid, outs), BF16),
             shape((towers, hid, outs), BF16),
+            shape((towers, total, outs), F32),
         ),
         in_specs=[vmem] * 4 + [anys] * 4 + [vmem] * 2,
-        out_specs=[vmem] * 2 + [anys] * 6,
+        out_specs=[vmem] * 2 + [anys] * 7,
         scratch_shapes=[
             pltpu.VMEM((towers, fin, hid), BF16),
             pltpu.VMEM((towers, fin, hid), BF16),
@@ -537,12 +567,13 @@
             pltpu.VMEM((towers, total, rows), BF16),
             pltpu.VMEM((n, total, lanes), F32),
             pltpu.VMEM((towers, max(total, fin), hid), F32),
+            pltpu.VMEM((towers, total, outs), F32),
             pltpu.VMEM((own, 3 * rank), F32),
             pltpu.VMEM((nt, piece, 3 * rank), F32),
             pltpu.VMEM((n, nt, piece, 3 * rank), F32),
             sem((2 * towers + 2,)),
-            sem((5,)),
-            sem((towers, total // chunk)),
+            sem((4 + towers + 1,)),
+            sem((towers,)),
             sem((3, n)),
             sem((n,)),
             sem((nt,)),
@@ -565,7 +596,7 @@
         lift,
         press,
         head[None, :],
-        label,
+        labels,
     )
     out = pl.pallas_call(
         functools.partial(update_kernel, (n, nt)),
@@ -576,15 +607,16 @@
             shape((block_hid, towers, outs), F32),
             shape((flat // n, rank), F32),
             shape((flat // n, rank), F32),
+            shape((1, piece), F32),
         ),
         grid=(1,),
-        in_specs=[vmem] * 2
+        in_specs=[vmem] * 4
         + [pl.BlockSpec((width, towers, hid), lambda i: (lax.axis_index("member"), 0, 0))]
         + [vmem] * 4
         + [anys] * 2
         + [vmem]
         + [anys] * 2,
-        out_specs=[vmem] * 6,
+        out_specs=[vmem] * 7,
         scratch_shapes=[
             pltpu.VMEM((flat, rank), F32),
             pltpu.VMEM((flat, rank), F32),
@@ -602,6 +634,8 @@
         ],
         compiler_params=pltpu.CompilerParams(vmem_limit_bytes=67043328),
     )(
+        logits,
+        tower_out,
         accumulator,
         decayed,
         first,
@@ -615,7 +649,7 @@
         hidden,
         counts,
     )
-    new_tables, new_acc, grad_first, grad_second, grad_lift, grad_press = out
+    new_tables, new_acc, grad_first, grad_second, grad_lift, grad_press, logits = out
     return (
         jnp.transpose(new_tables, (0, 2, 1))[:, None],
         new_acc,
@@ -623,7 +657,7 @@
         grad_second,
         grad_lift,
         grad_press,
-        logits[:, 0][None, :],
+        logits,
     )
 
 

time: 77.3 us -> 69.9 us (0.904)
  Pallas kernels: 73.7 us -> 68.9 us
  local copies, waits for them, and re-layouts: 1.99 us -> 0 us
    pallas_call x1, Pallas kernels: 22.2 us -> 17.6 us  [per_device(): pl.pallas_call(functools.partial(update_kernel, (n, nt)), out_shape=(shap...]
    slice x1 -> x0, local copies, waits for them, and re-layouts: 1.32 us -> none  [per_device(): logits[:, 0][None, :]]
where the time goes in v3:
time: 69.9 us; the launch traced here: 69.7 us
  Pallas kernels  68.9 us (99%)
  between operations  0.8 us (1%)
    pallas_call x1, Pallas kernels, per_device(): pl.pallas_call(functools.partial(gather_kernel, (n, nt)), out_shape=(shap...  51.4 us
    pallas_call x1, Pallas kernels, per_device(): pl.pallas_call(functools.partial(update_kernel, (n, nt)), out_shape=(shap...  17.6 us

profile of v3, /device:TPU:0, one launch (start us, length us, event | category | flops | bytes accessed | tf_op | source)
XLA Modules:
  0.0 69.7 jit_solution(13490456325366829938)
XLA Ops:
  0.6 51.4 %shard_map.162 = (f32[16,128]{1,0:T(8,128)}, f32[2,64,512]{2,1,0:T(8,128)}, f32[512,128]{1,0:T(8,128)}, f32[2,512,1024]{2,1,0:T(8,128)}, f32[8,4,16,384]{3,2,1,0...) custom-call(s32[2,4,512]{2,1,0:T(4,128)} %bitcast.13, ...), custom_call_target="tpu_custom_call" | custom-call | tf_op jit(solution)/shard_map/pallas_call | solution.py:543
  52.0 17.6 %shard_map.163 = (f32[2,64,512]{2,1,0:T(8,128)}, f32[2,1,512]{2,1,0:T(1,128)}, f32[64,2,1024]{2,1,0:T(2,128)}, f32[128,2,256]{2,1,0:T(2,128)}, f32[64,128]{1,0:T...) custom-call(f32[16,128]{1,0:T(8,128)} %get-tuple-element.23.logits_ref, f32[2,512,256]{2,1,0:T(8,128)} %get-tuple-element.24.tower_out_ref, ...), custom_call_target="tpu_custom_call" | custom-call | tf_op jit(solution)/shard_map/pallas_call | solution.py:601

commit v4 on v3

--- a/solution.py
+++ b/solution.py
@@ -69,6 +69,9 @@
     feats,
     hidden,
     tower_out,
+    own_feats,
+    oa_send,
+    oa_recv,
     stats,
     rs_buf,
     gath,
@@ -196,6 +199,20 @@
 
         block_copy(block, 2, me + 1 - 2 * core).wait_send()
 
+    def own_copy(d):
+        other = lax.rem(me + d, n)
+        return pltpu.make_async_remote_copy(
+            src_ref=feats.at[me, pl.ds(pl.multiple_of(other * own, own), own)],
+            dst_ref=own_feats.at[me],
+            send_sem=oa_send.at[d],
+            recv_sem=oa_recv.at[d],
+            device_id={"member": other},
+            device_id_type=MESH,
+        )
+
+    for d in range(1, n):
+        own_copy(d).start()
+    own_feats[me] = feats[me, pl.ds(pl.multiple_of(me * own, own), own), :]
     pass_on(me, True, True)
 
     stores = []
@@ -223,6 +240,70 @@
     store(w2h, w2h_out)
     store(w2l, w2l_out)
     store(feats.at[me], pooled_out)
+
+    head = head_ref[:, pl.ds(pl.multiple_of(tpos * flat, flat), flat)]
+
+    for d in range(1, n):
+        own_copy(d).wait_recv()
+    flat_out = []
+    for t in range(towers):
+        part = slice(t * width, (t + 1) * width)
+        x = jnp.concatenate([own_feats[j, :, part] for j in range(n)], axis=1)
+        h = dot3(split(x), (w1h[t], w1l[t]))
+        flat_out.append(dot3(split(h * sigmoid(h)), (w2h[t], w2l[t])))
+    flat_out = jnp.concatenate(flat_out, axis=1)
+    weighted = flat_out * head
+    stats[:, :rank] = dot3(split(flat_out), split(press[...]))
+    stats[:, rank : 2 * rank] = dot3(split(weighted), split(lift[...]))
+    stats[:, 2 * rank :] = jnp.broadcast_to(
+        jnp.sum(weighted, axis=1, keepdims=True), (own, rank)
+    )
+
+    def tower_copy(d):
+        other = lax.rem(tpos + d, nt)
+        return pltpu.make_async_remote_copy(
+            src_ref=stats.at[pl.ds(pl.multiple_of(other * piece, piece), piece)],
+            dst_ref=rs_buf.at[tpos],
+            send_sem=rs_send.at[d],
+            recv_sem=rs_recv.at[d],
+            device_id={"tower": other},
+            device_id_type=MESH,
+        )
+
+    for d in range(1, nt):
+        tower_copy(d).start()
+
+    def member_copy(d):
+        return pltpu.make_async_remote_copy(
+            src_ref=gath.at[me, tpos],
+            dst_ref=gath.at[me, tpos],
+            send_sem=gm_send.at[d],
+            recv_sem=gm_recv.at[d],
+            device_id={"member": lax.rem(me + d, n)},
+            device_id_type=MESH,
+        )
+
+    def settle():
+        for d in range(1, nt):
+            tower_copy(d).wait_recv()
+        summed = stats[pl.ds(pl.multiple_of(tpos * piece, piece), piece), :]
+        for d in range(1, nt):
+            summed = summed + rs_buf[lax.rem(tpos + d, nt)]
+        logit = (
+            jnp.sum(summed[:, :rank] * summed[:, rank : 2 * rank], axis=1, keepdims=True)
+            + summed[:, 2 * rank :]
+        )
+        logits_ref[...] = logit
+        place = lax.broadcasted_iota(jnp.int32, (piece, own), 1)
+        wanted = lax.broadcasted_iota(jnp.int32, (piece, own), 0) + tpos * piece
+        clicks = jnp.where(place == wanted, label_ref[...].astype(F32), 0.0)
+        error = sigmoid(logit) - jnp.sum(clicks, axis=1, keepdims=True)
+        gath[me, tpos, :, :rank] = error * summed[:, :rank]
+        gath[me, tpos, :, rank : 2 * rank] = error * summed[:, rank : 2 * rank]
+        gath[me, tpos, :, 2 * rank :] = error
+
+        for d in range(1, n):
+            member_copy(d).start()
 
     def accumulate(source, fresh):
         block_copy(2 * source + 1 - core, 0, me).wait_recv()
@@ -264,40 +345,14 @@
         def _():
             accumulate(chip + d, False)
 
+        if d == 1:
+            settle()
+
     def hidden_copy(t):
         return pltpu.make_async_copy(hidden.at[t, :total], hidden_out.at[t], hidden_sem.at[t])
 
     for t in range(towers):
         hidden_copy(t).start()
-
-    head = head_ref[:, pl.ds(pl.multiple_of(tpos * flat, flat), flat)]
-
-    mine = pl.ds(pl.multiple_of(me * own, own), own)
-    flat_out = []
-    for t in range(towers):
-        h = hidden[t, mine, :]
-        flat_out.append(dot3(split(h * sigmoid(h)), (w2h[t], w2l[t])))
-    flat_out = jnp.concatenate(flat_out, axis=1)
-    weighted = flat_out * head
-    stats[:, :rank] = dot3(split(flat_out), split(press[...]))
-    stats[:, rank : 2 * rank] = dot3(split(weighted), split(lift[...]))
-    stats[:, 2 * rank :] = jnp.broadcast_to(
-        jnp.sum(weighted, axis=1, keepdims=True), (own, rank)
-    )
-
-    def tower_copy(d):
-        other = lax.rem(tpos + d, nt)
-        return pltpu.make_async_remote_copy(
-            src_ref=stats.at[pl.ds(pl.multiple_of(other * piece, piece), piece)],
-            dst_ref=rs_buf.at[tpos],
-            send_sem=rs_send.at[d],
-            recv_sem=rs_recv.at[d],
-            device_id={"tower": other},
-            device_id_type=MESH,
-        )
-
-    for d in range(1, nt):
-        tower_copy(d).start()
 
     def tower_chunks(t):
         @pl.loop(0, total // chunk)
@@ -307,53 +362,6 @@
             tower_out[t, span, :] = dot3(split(h * sigmoid(h)), (w2h[t], w2l[t]))
 
         store(tower_out.at[t], tower_out_hbm.at[t])
-
-    tower_chunks(0)
-
-    for d in range(1, nt):
-        tower_copy(d).wait_recv()
-    summed = stats[pl.ds(pl.multiple_of(tpos * piece, piece), piece), :]
-    for d in range(1, nt):
-        summed = summed + rs_buf[lax.rem(tpos + d, nt)]
-    logit = (
-        jnp.sum(summed[:, :rank] * summed[:, rank : 2 * rank], axis=1, keepdims=True)
-        + summed[:, 2 * rank :]
-    )
-    logits_ref[...] = logit
-    place = lax.broadcasted_iota(jnp.int32, (piece, own), 1)
-    wanted = lax.broadcasted_iota(jnp.int32, (piece, own), 0) + tpos * piece
-    clicks = jnp.where(place == wanted, label_ref[...].astype(F32), 0.0)
-    error = sigmoid(logit) - jnp.sum(clicks, axis=1, keepdims=True)
-    gath[me, tpos, :, :rank] = error * summed[:, :rank]
-    gath[me, tpos, :, rank : 2 * rank] = error * summed[:, rank : 2 * rank]
-    gath[me, tpos, :, 2 * rank :] = error
-
-    def member_copy(d):
-        return pltpu.make_async_remote_copy(
-            src_ref=gath.at[me, tpos],
-            dst_ref=gath.at[me, tpos],
-            send_sem=gm_send.at[d],
-            recv_sem=gm_recv.at[d],
-            device_id={"member": lax.rem(me + d, n)},
-            device_id_type=MESH,
-        )
-
-    for d in range(1, n):
-        member_copy(d).start()
-    for t in range(1, towers):
-        tower_chunks(t)
-    for d in range(1, nt):
-        tower_copy(d).wait_send()
-    sent(me, True, True)
-    for d in range(1, chips):
-
-        @pl.when(chip >= d)
-        def _():
-            sent(me - 2 * d, True, False)
-
-        @pl.when(chip + d < chips)
-        def _():
-            sent(me + 2 * d, False, True)
 
     for d in range(1, n):
         member_copy(d).wait_recv()
@@ -370,9 +378,25 @@
 
     for d in range(1, nt):
         column_copy(d).start()
+    for t in range(towers):
+        tower_chunks(t)
     for d in range(1, nt):
         column_copy(d).wait_recv()
     store(gath, gath_out)
+    for d in range(1, n):
+        own_copy(d).wait_send()
+    for d in range(1, nt):
+        tower_copy(d).wait_send()
+    sent(me, True, True)
+    for d in range(1, chips):
+
+        @pl.when(chip >= d)
+        def _():
+            sent(me - 2 * d, True, False)
+
+        @pl.when(chip + d < chips)
+        def _():
+            sent(me + 2 * d, False, True)
     for d in range(1, n):
         member_copy(d).wait_send()
     for d in range(1, nt):
@@ -568,6 +592,9 @@
             pltpu.VMEM((n, total, lanes), F32),
             pltpu.VMEM((towers, max(total, fin), hid), F32),
             pltpu.VMEM((towers, total, outs), F32),
+            pltpu.VMEM((n, own, lanes), F32),
+            sem((n,)),
+            sem((n,)),
             pltpu.VMEM((own, 3 * rank), F32),
             pltpu.VMEM((nt, piece, 3 * rank), F32),
             pltpu.VMEM((n, nt, piece, 3 * rank), F32),

time: 69.9 us -> 69 us (0.987)
  Pallas kernels: 68.9 us -> 67.9 us
    pallas_call x1, Pallas kernels: 51.4 us -> 50.3 us  [per_device(): pl.pallas_call(functools.partial(gather_kernel, (n, nt)), out_shape=(shap...]
where the time goes in v4:
time: 69 us; the launch traced here: 68.7 us
  Pallas kernels  67.9 us (98%)
  between operations  0.8 us (1%)
    pallas_call x1, Pallas kernels, per_device(): pl.pallas_call(functools.partial(gather_kernel, (n, nt)), out_shape=(shap...  50.3 us
    pallas_call x1, Pallas kernels, per_device(): pl.pallas_call(functools.partial(update_kernel, (n, nt)), out_shape=(shap...  17.5 us

profile of v4, /device:TPU:0, one launch (start us, length us, event | category | flops | bytes accessed | tf_op | source)
XLA Modules:
  0.0 68.7 jit_solution(934717650065219760)
XLA Ops:
  0.6 50.3 %shard_map.162 = (f32[16,128]{1,0:T(8,128)}, f32[2,64,512]{2,1,0:T(8,128)}, f32[512,128]{1,0:T(8,128)}, f32[2,512,1024]{2,1,0:T(8,128)}, f32[8,4,16,384]{3,2,1,0...) custom-call(s32[2,4,512]{2,1,0:T(4,128)} %bitcast.13, ...), custom_call_target="tpu_custom_call" | custom-call | tf_op jit(solution)/shard_map/pallas_call | solution.py:567
  51.0 17.5 %shard_map.163 = (f32[2,64,512]{2,1,0:T(8,128)}, f32[2,1,512]{2,1,0:T(1,128)}, f32[64,2,1024]{2,1,0:T(2,128)}, f32[128,2,256]{2,1,0:T(2,128)}, f32[64,128]{1,0:T...) custom-call(f32[16,128]{1,0:T(8,128)} %get-tuple-element.23.logits_ref, f32[2,512,256]{2,1,0:T(8,128)} %get-tuple-element.24.tower_out_ref, ...), custom_call_target="tpu_custom_call" | custom-call | tf_op jit(solution)/shard_map/pallas_call | solution.py:628
